TPU v7x, 32 devices: a whole 2x2x4 slice. The times are simulated.
32 devices in a mesh: groups: 2 (over y), rows: 4 (over x, core), cols: 4 (over z).
Axes of the slice: x: 2, y: 2, z: 4, core: 2. Of those that a mesh axis runs over, the one named last changes fastest.
Arguments:
- pair_rep: float32 [384, 192, 128], P(('groups', 'cols'), 'rows'), parts along dimension 0, may hold values from -6 to 6
- token_mask: int32 [384], P(('groups', 'rows')), parts along dimension 0, may hold values from 0 to 1, as said below
- norm_gain: float32 [128], replicated, may hold values from 0.1 to 1.9
- norm_shift: float32 [128], replicated, may hold values from -3 to 3
- w_query: bfloat16 [128, 128], replicated, may hold values from -0.5 to 0.5
- w_keyval: bfloat16 [128, 256], replicated, may hold values from -0.5 to 0.5
- w_gate: bfloat16 [128, 128], replicated, may hold values from -0.5 to 0.5
- gate_shift: float32 [128], replicated, may hold values from -3 to 3
- w_bias: float32 [128, 4], replicated, may hold values from -12 to 12
- w_out: bfloat16 [128, 128], replicated, may hold values from -0.5 to 0.5
- out_shift: float32 [128], replicated, may hold values from -3 to 3
Outputs:
- pair_update: float32 [384, 192, 128], P(('groups', 'cols'), 'rows'), parts along dimension 0
There are 2 independent parts, one for each index of `groups`. A program takes and returns all parts, laid end to end along the dimension named above; an argument that names none is the same for every part. Nothing has to cross between parts.
Inputs may be any that keep to these rules, and one draw needn't show every extreme that they name: `token_mask`: position 0 is always a valid residue and the last position never is.
All inputs are finite; a program needn't handle non-finite values.
Results may differ from a plain program's by a relative error of at most 0.012.
The roundings to bfloat16 on the way count: a program that leaves them out, or rounds other values in their place, can miss the bound.
Values may be sent and summed in bfloat16 or wider, within the bound.
No kernel may reach another device: no remote copies, remote signals or barrier semaphores. Data moves between devices by JAX's collectives and lax.ppermute only.
A program may use at most 128 MiB of HBM per device.

v0:
```python
import jax
import jax.numpy as jnp
from jax import lax
from jax.sharding import PartitionSpec as P

HEADS = 4
HEAD_DIM = 32


def layer_norm(values, norm_gain, norm_shift):
    mean_val = jnp.mean(values, axis=-1, keepdims=True)
    centred = values - mean_val
    variance = jnp.mean(centred * centred, axis=-1, keepdims=True)
    return (centred * lax.rsqrt(variance + 1e-05) * norm_gain + norm_shift).astype(jnp.bfloat16)


def largest_divisor(count, limit):
    return max(
        (candidate for candidate in range(1, min(count, limit) + 1) if count % candidate == 0)
    )


def whole_row_layer(
    normed, token_mask, w_query, w_keyval, w_gate, gate_shift, w_bias, w_out, out_shift
):
    width = normed.shape[2]
    local_bias = jnp.dot(
        normed.astype(jnp.float32), w_bias, precision=lax.Precision.HIGHEST
    ).transpose(2, 0, 1)
    wide = lax.all_to_all(normed, "rows", split_axis=0, concat_axis=1, tiled=True)
    few_rows, token_count, _ = wide.shape
    bias_part = lax.all_gather(local_bias, "cols", axis=1, tiled=True)
    full_bias, full_mask = (
        lax.all_gather(bias_part, "rows", axis=2, tiled=True),
        lax.all_gather(token_mask.astype(jnp.float32), "rows", axis=0, tiled=True),
    )
    queries = (
        jnp.dot(wide, w_query, preferred_element_type=jnp.float32) * HEAD_DIM ** (-0.5)
    ).astype(jnp.bfloat16)
    queries = queries.reshape(few_rows, token_count, HEADS, HEAD_DIM)
    keyvals = jnp.dot(wide, w_keyval, preferred_element_type=jnp.float32).astype(jnp.bfloat16)
    keys = keyvals[..., :width].reshape(few_rows, token_count, HEADS, HEAD_DIM)
    values = keyvals[..., width:].reshape(few_rows, token_count, HEADS, HEAD_DIM)
    gates = jax.nn.sigmoid(jnp.dot(wide, w_gate, preferred_element_type=jnp.float32) + gate_shift)
    usable = full_mask > 0.5
    block_len = largest_divisor(token_count, 128)

    def one_block(block_index, gated_all):
        start = block_index * block_len
        query_block = lax.dynamic_slice_in_dim(queries, start, block_len, 1)
        bias_block = lax.dynamic_slice_in_dim(full_bias, start, block_len, 1)
        gate_block = lax.dynamic_slice_in_dim(gates, start, block_len, 1)
        scores = jnp.einsum(
            "ijhd,ikhd->hijk", query_block, keys, preferred_element_type=jnp.float32
        )
        scores = scores + bias_block[:, None]
        scores = jnp.where(usable[None, None, None, :], scores, jnp.float32(-1000000000.0))
        highest = jnp.max(scores, axis=-1, keepdims=True)
        expo = jnp.exp(scores - highest)
        total = jnp.sum(expo, axis=-1)
        weights = expo.astype(jnp.bfloat16)
        mixed = jnp.einsum("hijk,ikhd->ijhd", weights, values, preferred_element_type=jnp.float32)
        attended = mixed / total.transpose(1, 2, 0)[..., None]
        gated = (gate_block * attended.reshape(few_rows, block_len, width)).astype(jnp.bfloat16)
        return lax.dynamic_update_slice_in_dim(gated_all, gated, start, 1)

    gated_all = lax.fori_loop(
        0,
        token_count // block_len,
        one_block,
        jnp.zeros((few_rows, token_count, width), jnp.bfloat16),
    )
    gated_home = lax.all_to_all(gated_all, "rows", split_axis=1, concat_axis=0, tiled=True)
    return jnp.dot(gated_home, w_out, preferred_element_type=jnp.float32) + out_shift


def on_device(
    pair_rep,
    token_mask,
    norm_gain,
    norm_shift,
    w_query,
    w_keyval,
    w_gate,
    gate_shift,
    w_bias,
    w_out,
    out_shift,
):
    normed = layer_norm(pair_rep, norm_gain, norm_shift)
    return whole_row_layer(
        normed, token_mask, w_query, w_keyval, w_gate, gate_shift, w_bias, w_out, out_shift
    )


def solution(mesh):
    return jax.shard_map(
        on_device,
        mesh=mesh,
        in_specs=(
            P(("groups", "cols"), "rows", None),
            P(("groups", "rows")),
            P(),
            P(),
            P(),
            P(),
            P(),
            P(),
            P(),
            P(),
            P(),
        ),
        out_specs=P(("groups", "cols"), "rows", None),
        check_vma=False,
    )
```

profile of v0, /device:TPU:0, one launch (start us, length us, event | category | flops | bytes accessed | tf_op | source)
XLA Modules:
  0.0 85.9 jit_solution(3610924705760710887)
XLA Ops:
  0.0 0.0 copy-start
  0.0 1.7 %reduce_sum.31 = f32[48,48]{1,0:T(8,128)S(1)} reduce(f32[48,48,128]{2,1,0:T(8,128)} %param.13, f32[]{:T(128)} %constant.58.clone.1), dimensions={2}, to_apply=%region_0.0 | reduce | flops 292608 | bytes 1188868 | tf_op jit(solution)/shard_map/reduce_sum | solution.py:11
  1.8 0.0 copy-done.1
  1.8 0.7 multiply_reduce_fusion
  2.5 0.0 copy-done.9
  2.5 0.0 copy-done.8
  2.5 0.0 copy-start.7
  2.5 1.5 %add_convert_fusion = bf16[48,48,128]{2,1,0:T(8,128)(2,1)} fusion(f32[48,48,128]{2,1,0:T(8,128)S(1)} %copy-done.1, f32[128]{0:T(128)S(1)} %copy-done.8, f32[128]{0:T(128)S(1)} %copy-done.9, f32[48,48]{1,0:T(8,128)S(1)} %add_rsqrt_fusion, f32[48,48]{1,0:T(8,128)S(1)} %broadcast_multiply_fusion), kind=kLoop, calls=%fused_computation.31 | loop fusion | flops 1474560 | bytes 1788928 | tf_op jit(solution)/shard_map/convert_element_type | solution.py:14
  4.0 4.2 %all-to-all-start = ((bf16[48,48,128]{2,1,0:T(8,128)(2,1)}), bf16[48,48,128]{2,1,0:T(8,128)(2,1)S(1)}, u32[]{:S(2)}, u32[]{:S(2)}) async-start(bf16[48,48,128]{2,1,0:T(8,128)(2,1)} %add_convert_fusion), calls=%async_computation | async-start | bytes 1179648 | tf_op jit(solution)/shard_map/all_to_all | solution.py:30
  8.3 0.0 copy-done.7
  8.3 2.8 %convolution_bitcast_fusion = f32[4,48,48]{2,0,1:T(4,128)S(1)} fusion(bf16[48,48,128]{2,1,0:T(8,128)(2,1)} %add_convert_fusion, f32[128,4]{0,1:T(4,128)S(1)} %copy-done.7), kind=kOutput, calls=%fused_computation.33 | convolution fusion | flops 14155776 | bytes 628736 | tf_op jit(solution)/shard_map/dot_general | solution.py:27
  11.1 15.8 %all_gather.10 = f32[4,192,48]{2,0,1:T(4,128)S(1)} all-gather(f32[4,48,48]{2,0,1:T(4,128)S(1)} %convolution_bitcast_fusion), channel_id=1, replica_groups=mesh['groups'=2,'rows'=4,'cols'=4] {'cols'}, dimensions={1}, use_global_device_ids=true | all-gather | bytes 184320 | tf_op jit(solution)/shard_map/all_gather | solution.py:32
  27.0 0.2 copy.36
  27.2 0.0 copy-done.14
  27.2 0.6 dynamic-slice
  28.3 0.0 copy-done.12
  28.3 0.1 convert_dynamic-update-slice_fusion
  28.4 5.6 %all-reduce = f32[192]{0:T(256)S(1)} all-reduce(f32[192]{0:T(256)S(1)} %convert_dynamic-update-slice_fusion), channel_id=1, replica_groups=mesh['groups'=2,'rows'=4,'cols'=4] {'rows'}, use_global_device_ids=true, to_apply=%add | all-reduce | flops 192 | bytes 1536
  34.1 9.0 %all_gather.11 = f32[4,192,192]{1,0,2:T(4,128)S(1)} all-gather(f32[4,192,48]{1,0,2:T(4,128)S(1)} %copy.36), channel_id=1, replica_groups=mesh['groups'=2,'rows'=4,'cols'=4] {'rows'}, dimensions={2}, use_global_device_ids=true | all-gather | bytes 737280 | tf_op jit(solution)/shard_map/all_gather | solution.py:34
  43.1 0.0 all-to-all-done
  43.1 0.1 copy.33
  43.2 0.0 copy-done
  43.2 0.4 convolution_convert_fusion
  43.7 0.3 fusion.39
  44.0 0.3 copy.35
  44.3 0.0 copy-start.6
  44.3 0.9 %copy.40 = bf16[12,192,4,32]{1,3,0,2:T(8,128)(2,1)} copy(bf16[12,192,4,32]{1,3,2,0:T(8,128)(2,1)S(1)} %bitcast.59) | data formatting | bytes 1179648 | tf_op jit(solution)/shard_map/while | solution.py:67
  45.2 1.2 %copy.37 = bf16[12,192,128]{1,2,0:T(8,128)(2,1)} copy(bf16[12,192,128]{2,1,0:T(8,128)(2,1)S(1)} %get-tuple-element.188) | data formatting | bytes 1179648 | tf_op jit(solution)/shard_map/slice | solution.py:43
  46.4 0.0 copy-done.6
  46.4 0.3 fusion.28
  46.7 1.2 %copy.34 = bf16[12,192,128]{1,2,0:T(8,128)(2,1)} copy(bf16[12,192,128]{2,1,0:T(8,128)(2,1)S(1)} %fusion.28) | data formatting | bytes 1179648 | tf_op jit(solution)/shard_map/convert_element_type | solution.py:39
  47.9 0.0 copy-done.11
  47.9 0.0 copy-done.13
  47.9 1.5 %fusion.27 = f32[12,192,128]{2,1,0:T(8,128)} fusion(bf16[12,192,128]{2,1,0:T(8,128)(2,1)S(1)} %bitcast.58, f32[128]{0:T(128)S(1)} %copy-done.13, bf16[128,128]{1,0:T(8,128)(2,1)S(1)} %copy-done.11), kind=kOutput, calls=%fused_computation.29 | convolution fusion | flops 76677120 | bytes 1802752 | tf_op jit(solution)/shard_map/dot_general | solution.py:44
  49.3 1.0 %broadcast_in_dim.45.clone = bf16[12,192,128]{2,0,1:T(8,128)(2,1)} broadcast(bf16[]{:T(256)} %constant.57.clone.1), dimensions={} | broadcast | bytes 589826 | tf_op jit(solution)/shard_map/broadcast_in_dim | solution.py:71
  50.3 0.0 copy-done.3
  50.3 18.9 %while.13 = (s32[]{:T(128)}, bf16[12,192,128]{2,0,1:T(8,128)(2,1)}, f32[12,192,128]{2,1,0:T(8,128)}, pred[192]{0:T(512)(128)(4,1)S(1)}, bf16[12,192,4,32]{1,3,2,...) while((s32[]{:T(128)}, bf16[12,192,128]{2,0,1:T(8,128)(2,1)}, ...), condition=%wide.region_5.6_spmd, body=%wide.region_2.5_spmd.sunk | while | flops 118112448 | bytes 19440052 | solution.py:67
  50.3 0.3 constant_dynamic-slice_fusion.13
  50.6 0.2 copy.78
  50.8 4.4 %fusion.59 = (f32[4,12,96]{2,1,0:T(8,128)S(1)}, bf16[4,12,96,192]{3,2,1,0:T(8,128)(2,1)}) fusion(f32[4,96,192]{2,1,0:T(8,128)S(1)} %copy.78, pred[192]{0:T(512)(128)(4,1)S(1)} %get-tuple-element.270, bf16[12,192,4,32]{1,3,0,2:T(8,128)(2,1)S(1)} %get-tuple-element.272, bf16[12,192,4,32]{1,3,2,0:T(8,128)(2,1)} %get-tuple-element.271, s32[]{:T(128)S(6)} %select_n.31), kind=kOutput, calls=%fused_computation.43.clone.1 | convolution fusion | flops 61046976 | bytes 3066052 | tf_op jit(solution)/shard_map/while/body/eval_jaxpr/sub | solution.py:59
  55.3 0.0 copy-start.2
  55.3 2.9 %fusion.60 = f32[12,96,4,32]{1,3,2,0:T(8,128)S(1)} fusion(bf16[12,192,4,32]{1,3,2,0:T(8,128)(2,1)} %get-tuple-element.274, bf16[4,12,96,192]{3,2,1,0:T(8,128)(2,1)} %get-tuple-element.241, f32[12,96,4]{1,2,0:T(4,128)S(1)} %copy.79), kind=kOutput, calls=%fused_computation.10.clone.1 | convolution fusion | flops 56770560 | bytes 2967552 | tf_op jit(solution)/shard_map/while/body/eval_jaxpr/hijk,ikhd->ijhd/dot_general | solution.py:62
  58.2 0.0 copy-done.2
  58.2 0.1 constant_dynamic-slice_fusion.12
  58.3 0.3 copy.77
  58.5 0.1 fusion.61
  58.6 0.0 copy-start.4
  58.6 0.3 copy.80
  59.0 0.8 constant_dynamic-update-slice_fusion.2
  59.8 0.0 copy-done.4
  59.8 0.3 constant_dynamic-slice_fusion.13
  60.1 0.2 copy.78
  60.3 4.4 %fusion.59 = (f32[4,12,96]{2,1,0:T(8,128)S(1)}, bf16[4,12,96,192]{3,2,1,0:T(8,128)(2,1)}) fusion(f32[4,96,192]{2,1,0:T(8,128)S(1)} %copy.78, pred[192]{0:T(512)(128)(4,1)S(1)} %get-tuple-element.270, bf16[12,192,4,32]{1,3,0,2:T(8,128)(2,1)S(1)} %get-tuple-element.272, bf16[12,192,4,32]{1,3,2,0:T(8,128)(2,1)} %get-tuple-element.271, s32[]{:T(128)S(6)} %select_n.31), kind=kOutput, calls=%fused_computation.43.clone.1 | convolution fusion | flops 61046976 | bytes 3066052 | tf_op jit(solution)/shard_map/while/body/eval_jaxpr/sub | solution.py:59
  64.7 0.0 copy-start.2
  64.7 2.9 %fusion.60 = f32[12,96,4,32]{1,3,2,0:T(8,128)S(1)} fusion(bf16[12,192,4,32]{1,3,2,0:T(8,128)(2,1)} %get-tuple-element.274, bf16[4,12,96,192]{3,2,1,0:T(8,128)(2,1)} %get-tuple-element.241, f32[12,96,4]{1,2,0:T(4,128)S(1)} %copy.79), kind=kOutput, calls=%fused_computation.10.clone.1 | convolution fusion | flops 56770560 | bytes 2967552 | tf_op jit(solution)/shard_map/while/body/eval_jaxpr/hijk,ikhd->ijhd/dot_general | solution.py:62
  67.6 0.1 constant_dynamic-slice_fusion.12
  67.7 0.3 copy.77
  68.0 0.1 fusion.61
  68.1 0.3 copy.80
  68.4 0.8 constant_dynamic-update-slice_fusion.2
  69.2 0.0 copy-done.4
  69.2 15.2 %all_to_all.36 = bf16[12,192,128]{2,0,1:T(8,128)(2,1)S(1)} all-to-all(bf16[12,192,128]{2,0,1:T(8,128)(2,1)} %get-tuple-element.281), channel_id=1, replica_groups=mesh['groups'=2,'rows'=4,'cols'=4] {'rows'}, dimensions={1} | all-to-all | bytes 1179648 | tf_op jit(solution)/shard_map/all_to_all | solution.py:73
  84.4 0.2 copy.44
  84.6 1.3 %convolution_add_fusion = f32[48,48,128]{2,1,0:T(8,128)} fusion(bf16[48,48,128]{2,1,0:T(8,128)(2,1)S(1)} %bitcast.62, f32[128]{0:T(128)S(1)} %copy-done.10, bf16[128,128]{1,0:T(8,128)(2,1)S(1)} %copy-done.5), kind=kOutput, calls=%fused_computation.23 | convolution fusion | flops 75792384 | bytes 1802752 | tf_op jit(solution)/shard_map/dot_general | solution.py:74
  (20 shorter events, 0.1 us)
Async XLA Ops:
  0.0 43.2 %copy-start = (bf16[128,256]{1,0:T(8,128)(2,1)S(1)}, bf16[128,256]{1,0:T(8,128)(2,1)}, u32[]{:S(2)}) copy-start(bf16[128,256]{1,0:T(8,128)(2,1)} %param.18) | copy-start | bytes 196612
  0.0 1.8 %copy-start.1 = (f32[48,48,128]{2,1,0:T(8,128)S(1)}, f32[48,48,128]{2,1,0:T(8,128)}, u32[]{:S(2)}) copy-start(f32[48,48,128]{2,1,0:T(8,128)} %param.13) | copy-start | bytes 3538948
  0.0 2.5 %copy-start.9 = (f32[128]{0:T(128)S(1)}, f32[128]{0:T(128)}, u32[]{:S(2)}) copy-start(f32[128]{0:T(128)} %param.15) | copy-start | bytes 1540
  0.0 2.5 %copy-start.8 = (f32[128]{0:T(128)S(1)}, f32[128]{0:T(128)}, u32[]{:S(2)}) copy-start(f32[128]{0:T(128)} %param.16) | copy-start | bytes 1540
  2.5 5.8 %copy-start.7 = (f32[128,4]{0,1:T(4,128)S(1)}, f32[128,4]{0,1:T(4,128)}, u32[]{:S(2)}) copy-start(f32[128,4]{0,1:T(4,128)} %param.21) | copy-start | bytes 6148
  4.0 39.1 %all-to-all-start = ((bf16[48,48,128]{2,1,0:T(8,128)(2,1)}), bf16[48,48,128]{2,1,0:T(8,128)(2,1)S(1)}, u32[]{:S(2)}, u32[]{:S(2)}) async-start(bf16[48,48,128]{2,1,0:T(8,128)(2,1)} %add_convert_fusion), calls=%async_computation | async-start | bytes 1179648 | tf_op jit(solution)/shard_map/all_to_all | solution.py:30
  8.3 18.9 %copy-start.14 = (u32[32]{0:T(128)S(1)}, u32[32]{0:T(128)}, u32[]{:S(2)}) copy-start(u32[32]{0:T(128)} %constant.66) | copy-start | bytes 388
  8.3 20.1 %copy-start.12 = (s32[48]{0:T(128)S(1)}, s32[48]{0:T(128)}, u32[]{:S(2)}) copy-start(s32[48]{0:T(128)} %param.14) | copy-start | bytes 580
  44.3 2.1 %copy-start.6 = (bf16[128,128]{1,0:T(8,128)(2,1)S(1)}, bf16[128,128]{1,0:T(8,128)(2,1)}, u32[]{:S(2)}) copy-start(bf16[128,128]{1,0:T(8,128)(2,1)} %param.17) | copy-start | bytes 98308
  46.4 1.5 %copy-start.11 = (bf16[128,128]{1,0:T(8,128)(2,1)S(1)}, bf16[128,128]{1,0:T(8,128)(2,1)}, u32[]{:S(2)}) copy-start(bf16[128,128]{1,0:T(8,128)(2,1)} %param.19) | copy-start | bytes 98308
  46.4 1.5 %copy-start.13 = (f32[128]{0:T(128)S(1)}, f32[128]{0:T(128)}, u32[]{:S(2)}) copy-start(f32[128]{0:T(128)} %param.20) | copy-start | bytes 1540
  47.9 2.5 %copy-start.3 = (bf16[12,192,4,32]{1,3,0,2:T(8,128)(2,1)S(1)}, bf16[12,192,4,32]{1,3,0,2:T(8,128)(2,1)}, u32[]{:S(2)}) copy-start(bf16[12,192,4,32]{1,3,0,2:T(8,128)(2,1)} %copy.40) | copy-start | bytes 1769476
  55.3 2.9 %copy-start.2 = (f32[12,192,128]{2,1,0:T(8,128)S(1)}, f32[12,192,128]{2,1,0:T(8,128)}, u32[]{:S(2)}) copy-start(f32[12,192,128]{2,1,0:T(8,128)} %get-tuple-element.269) | copy-start | bytes 3538948 | tf_op jit(solution)/shard_map/while
  58.6 1.2 %copy-start.4 = (bf16[12,192,4,32]{1,3,0,2:T(8,128)(2,1)S(1)}, bf16[12,192,4,32]{1,3,0,2:T(8,128)(2,1)}, u32[]{:S(2)}) copy-start(bf16[12,192,4,32]{1,3,0,2:T(8,128)(2,1)} %get-tuple-element.292) | copy-start | bytes 1769476 | tf_op jit(solution)/shard_map/while
  64.7 2.9 %copy-start.2 = (f32[12,192,128]{2,1,0:T(8,128)S(1)}, f32[12,192,128]{2,1,0:T(8,128)}, u32[]{:S(2)}) copy-start(f32[12,192,128]{2,1,0:T(8,128)} %get-tuple-element.269) | copy-start | bytes 3538948 | tf_op jit(solution)/shard_map/while
  68.1 1.1 %copy-start.4 = (bf16[12,192,4,32]{1,3,0,2:T(8,128)(2,1)S(1)}, bf16[12,192,4,32]{1,3,0,2:T(8,128)(2,1)}, u32[]{:S(2)}) copy-start(bf16[12,192,4,32]{1,3,0,2:T(8,128)(2,1)} %get-tuple-element.292) | copy-start | bytes 1769476 | tf_op jit(solution)/shard_map/while
  69.2 15.4 %copy-start.5 = (bf16[128,128]{1,0:T(8,128)(2,1)S(1)}, bf16[128,128]{1,0:T(8,128)(2,1)}, u32[]{:S(2)}) copy-start(bf16[128,128]{1,0:T(8,128)(2,1)} %param.22) | copy-start | bytes 98308
  69.2 15.4 %copy-start.10 = (f32[128]{0:T(128)S(1)}, f32[128]{0:T(128)}, u32[]{:S(2)}) copy-start(f32[128]{0:T(128)} %param.23) | copy-start | bytes 1540
where the time goes:
time: 86.4 us; the launch traced here: 85.9 us
  blocking collectives  45.7 us (53%)
  matrix products  21 us (24%)
  local copies, waits for them, and re-layouts  9.81 us (11%)
  other arithmetic  4.24 us (5%)
  starting transfers between devices  4.24 us (5%)
    all_gather x1, blocking collectives, whole_row_layer(): bias_part = lax.all_gather(local_bias, 'cols', axis=1, tiled=True)  15.8 us
    all_to_all x1, blocking collectives, whole_row_layer(): lax.all_to_all(gated_all, 'rows', split_axis=1, concat_axis=0, tiled=True)  15.2 us
    all_gather x1, blocking collectives, whole_row_layer(): lax.all_gather(bias_part, 'rows', axis=2, tiled=True)  9.04 us
    sub x2, matrix products, one_block(): expo = jnp.exp(scores - highest)  8.86 us
    dot_general x2, matrix products, one_block(): jnp.einsum('hijk,ikhd->ijhd', weights, values, preferred_element_type=jnp...  5.81 us
    unnamed x1, blocking collectives  5.63 us
    all_to_all x1, starting transfers between devices, whole_row_layer(): lax.all_to_all(normed, 'rows', split_axis=0, concat_axis=1, tiled=True)  4.24 us
    dot_general x1, matrix products, whole_row_layer(): jnp.dot(normed.astype(jnp.float32), w_bias, precision=lax.Precision.HIGHEST)  2.85 us
  transfers between devices with their start and end apart: 1, of which 0 were waited for; matrix products, arithmetic and copies ran while one was open for 4% of the time, Pallas kernels for 0%

commit v1 on v0

--- a/solution.py
+++ b/solution.py
@@ -31,7 +31,9 @@
     few_rows, token_count, _ = wide.shape
     bias_part = lax.all_gather(local_bias, "cols", axis=1, tiled=True)
     full_bias, full_mask = (
-        lax.all_gather(bias_part, "rows", axis=2, tiled=True),
+        jnp.concatenate(
+            lax.all_to_all(jnp.stack([bias_part] * lax.axis_size("rows")), "rows", 0, 0), axis=2
+        ),
         lax.all_gather(token_mask.astype(jnp.float32), "rows", axis=0, tiled=True),
     )
     queries = (

time: 86.4 us -> 87.3 us (1.010)
  blocking collectives: 45.7 us -> 36.7 us
  starting transfers between devices: 4.24 us -> 7.74 us
  waiting for transfers between devices: 0.01 us -> 3.47 us
  local copies, waits for them, and re-layouts: 9.81 us -> 12.5 us
    all_gather x1 -> x0, blocking collectives: 9.04 us -> none  [whole_row_layer(): lax.all_gather(bias_part, 'rows', axis=2, tiled=True)]
    all_to_all x0 -> x1, starting transfers between devices: none -> 3.49 us  [whole_row_layer(): lax.all_to_all(jnp.stack([bias_part] * lax.axis_size('rows')), 'rows', 0, 0)]
    all_to_all x0 -> x1, waiting for transfers between devices: none -> 3.47 us  [whole_row_layer(): lax.all_to_all(jnp.stack([bias_part] * lax.axis_size('rows')), 'rows', 0, 0)]
    slice x1, local copies, waits for them, and re-layouts: 0.28 us -> 1.33 us  [whole_row_layer(): keys = keyvals[..., :width].reshape(few_rows, token_count, HEADS, HEAD_DIM)]
    another operation x0 -> x1, local copies, waits for them, and re-layouts: none -> 0.96 us  [whole_row_layer(): jnp.stack([bias_part] * lax.axis_size('rows'))]
  transfers between devices with their start and end apart: 1 -> 2, of which waited for: 0 -> 1; matrix products, arithmetic and copies ran while one was open for 4% -> 14% of each run, Pallas kernels for 0% -> 0%
where the time goes in v1:
time: 87.3 us; the launch traced here: 86.7 us
  blocking collectives  36.7 us (42%)
  matrix products  21.1 us (24%)
  local copies, waits for them, and re-layouts  12.5 us (14%)
  starting transfers between devices  7.74 us (9%)
  other arithmetic  4.24 us (5%)
  waiting for transfers between devices  3.47 us (4%)
    all_gather x1, blocking collectives, whole_row_layer(): bias_part = lax.all_gather(local_bias, 'cols', axis=1, tiled=True)  15.8 us
    all_to_all x1, blocking collectives, whole_row_layer(): lax.all_to_all(gated_all, 'rows', split_axis=1, concat_axis=0, tiled=True)  15.2 us
    sub x2, matrix products, one_block(): expo = jnp.exp(scores - highest)  8.96 us
    dot_general x2, matrix products, one_block(): jnp.einsum('hijk,ikhd->ijhd', weights, values, preferred_element_type=jnp...  5.81 us
    unnamed x1, blocking collectives  5.63 us
    all_to_all x1, starting transfers between devices, whole_row_layer(): lax.all_to_all(normed, 'rows', split_axis=0, concat_axis=1, tiled=True)  4.24 us
    all_to_all x1, starting transfers between devices, whole_row_layer(): lax.all_to_all(jnp.stack([bias_part] * lax.axis_size('rows')), 'rows', 0, 0)  3.49 us
    all_to_all x1, waiting for transfers between devices, whole_row_layer(): lax.all_to_all(jnp.stack([bias_part] * lax.axis_size('rows')), 'rows', 0, 0)  3.47 us
  transfers between devices with their start and end apart: 2, of which 1 were waited for; matrix products, arithmetic and copies ran while one was open for 14% of the time, Pallas kernels for 0%

profile of v1, /device:TPU:0, one launch (start us, length us, event | category | flops | bytes accessed | tf_op | source)
XLA Modules:
  0.0 86.7 jit_solution(13453615707136362202)
XLA Ops:
  0.0 0.0 copy-start
  0.0 1.7 %reduce_sum.31 = f32[48,48]{1,0:T(8,128)S(1)} reduce(f32[48,48,128]{2,1,0:T(8,128)} %param.13, f32[]{:T(128)} %constant.58.clone.1), dimensions={2}, to_apply=%region_0.0 | reduce | flops 292608 | bytes 1188868 | tf_op jit(solution)/shard_map/reduce_sum | solution.py:11
  1.8 0.0 copy-done.1
  1.8 0.7 multiply_reduce_fusion
  2.5 0.0 copy-done.9
  2.5 0.0 copy-done.8
  2.5 0.0 copy-start.7
  2.5 1.5 %add_convert_fusion = bf16[48,48,128]{2,1,0:T(8,128)(2,1)} fusion(f32[48,48,128]{2,1,0:T(8,128)S(1)} %copy-done.1, f32[128]{0:T(128)S(1)} %copy-done.8, f32[128]{0:T(128)S(1)} %copy-done.9, f32[48,48]{1,0:T(8,128)S(1)} %add_rsqrt_fusion, f32[48,48]{1,0:T(8,128)S(1)} %broadcast_multiply_fusion), kind=kLoop, calls=%fused_computation.31 | loop fusion | flops 1474560 | bytes 1788928 | tf_op jit(solution)/shard_map/convert_element_type | solution.py:14
  4.0 4.2 %all-to-all-start = ((bf16[48,48,128]{2,1,0:T(8,128)(2,1)}), bf16[48,48,128]{2,1,0:T(8,128)(2,1)S(1)}, u32[]{:S(2)}, u32[]{:S(2)}) async-start(bf16[48,48,128]{2,1,0:T(8,128)(2,1)} %add_convert_fusion), calls=%async_computation | async-start | bytes 1179648 | tf_op jit(solution)/shard_map/all_to_all | solution.py:30
  8.3 0.0 copy-done.7
  8.3 2.8 %convolution_bitcast_fusion = f32[4,48,48]{2,0,1:T(4,128)S(1)} fusion(bf16[48,48,128]{2,1,0:T(8,128)(2,1)} %add_convert_fusion, f32[128,4]{0,1:T(4,128)S(1)} %copy-done.7), kind=kOutput, calls=%fused_computation.33 | convolution fusion | flops 14155776 | bytes 628736 | tf_op jit(solution)/shard_map/dot_general | solution.py:27
  11.1 15.8 %all_gather.7 = f32[4,192,48]{2,0,1:T(4,128)S(1)} all-gather(f32[4,48,48]{2,0,1:T(4,128)S(1)} %convolution_bitcast_fusion), channel_id=1, replica_groups=mesh['groups'=2,'rows'=4,'cols'=4] {'cols'}, dimensions={1}, use_global_device_ids=true | all-gather | bytes 184320 | tf_op jit(solution)/shard_map/all_gather | solution.py:32
  27.0 0.2 copy.37
  27.1 0.0 copy-done.14
  27.2 0.6 dynamic-slice
  28.3 0.0 copy-done.12
  28.3 0.1 convert_dynamic-update-slice_fusion
  28.4 5.6 %all-reduce = f32[192]{0:T(256)S(1)} all-reduce(f32[192]{0:T(256)S(1)} %convert_dynamic-update-slice_fusion), channel_id=1, replica_groups=mesh['groups'=2,'rows'=4,'cols'=4] {'rows'}, use_global_device_ids=true, to_apply=%add | all-reduce | flops 192 | bytes 1536
  34.1 0.0 all-to-all-done
  34.1 1.0 %stack.2 = f32[4,4,192,48]{2,3,1,0:T(8,128)} broadcast(f32[4,192,48]{1,2,0:T(8,128)S(1)} %copy.37), dimensions={1,2,3} | broadcast | bytes 737280 | tf_op jit(solution)/shard_map/stack | solution.py:35
  35.0 3.5 %all-to-all-start.1 = ((f32[4,4,192,48]{2,3,1,0:T(8,128)}), f32[4,4,192,48]{2,3,1,0:T(8,128)S(1)}, u32[]{:S(2)}, u32[]{:S(2)}) async-start(f32[4,4,192,48]{2,3,1,0:T(8,128)} %stack.2), calls=%async_computation.1 | async-start | bytes 1572864 | tf_op jit(solution)/shard_map/all_to_all | solution.py:35
  38.5 0.1 copy.34
  38.6 0.0 copy-done
  38.6 0.4 convolution_convert_fusion
  39.0 1.1 %fusion.39 = (bf16[12,192,128]{2,1,0:T(8,128)(2,1)S(1)}, bf16[12,192,128]{2,1,0:T(8,128)(2,1)}) fusion(bf16[12,192,256]{2,1,0:T(8,128)(2,1)S(1)} %convolution_convert_fusion), kind=kLoop, calls=%fused_computation.44 | loop fusion | bytes 2359296 | tf_op jit(solution)/shard_map/slice | solution.py:45
  40.2 1.3 %copy.36 = bf16[12,192,128]{1,2,0:T(8,128)(2,1)S(1)} copy(bf16[12,192,128]{2,1,0:T(8,128)(2,1)} %get-tuple-element.189) | data formatting | bytes 1179648 | tf_op jit(solution)/shard_map/slice | solution.py:44
  41.5 0.0 copy-start.6
  41.5 0.9 %copy.42 = bf16[12,192,4,32]{1,3,0,2:T(8,128)(2,1)} copy(bf16[12,192,4,32]{1,3,2,0:T(8,128)(2,1)S(1)} %bitcast.63) | data formatting | bytes 1179648 | tf_op jit(solution)/shard_map/while | solution.py:69
  42.5 1.2 %copy.39 = bf16[12,192,128]{1,2,0:T(8,128)(2,1)} copy(bf16[12,192,128]{2,1,0:T(8,128)(2,1)S(1)} %get-tuple-element.188) | data formatting | bytes 1179648 | tf_op jit(solution)/shard_map/slice | solution.py:45
  43.7 0.0 copy-done.6
  43.7 0.3 fusion.28
  44.0 1.2 %copy.35 = bf16[12,192,128]{1,2,0:T(8,128)(2,1)} copy(bf16[12,192,128]{2,1,0:T(8,128)(2,1)S(1)} %fusion.28) | data formatting | bytes 1179648 | tf_op jit(solution)/shard_map/convert_element_type | solution.py:41
  45.2 0.0 copy-done.11
  45.2 0.0 copy-done.13
  45.2 1.5 %fusion.27 = f32[12,192,128]{2,1,0:T(8,128)} fusion(bf16[12,192,128]{2,1,0:T(8,128)(2,1)S(1)} %bitcast.62, f32[128]{0:T(128)S(1)} %copy-done.13, bf16[128,128]{1,0:T(8,128)(2,1)S(1)} %copy-done.11), kind=kOutput, calls=%fused_computation.29 | convolution fusion | flops 76677120 | bytes 1802752 | tf_op jit(solution)/shard_map/dot_general | solution.py:46
  46.6 3.5 %all-to-all-done.1 = f32[4,4,192,48]{2,3,1,0:T(8,128)S(1)} async-done(((f32[4,4,192,48]{2,3,1,0:T(8,128)}), f32[4,4,192,48]{2,3,1,0:T(8,128)S(1)}, u32[]{:S(2)}, u32[]{:S(2)}) %all-to-all-start.1) | async-done | bytes 589856 | tf_op jit(solution)/shard_map/all_to_all | solution.py:35
  50.1 0.1 copy.38
  50.2 1.0 %broadcast_in_dim.45.clone = bf16[12,192,128]{2,0,1:T(8,128)(2,1)} broadcast(bf16[]{:T(256)} %constant.57.clone.1), dimensions={} | broadcast | bytes 589826 | tf_op jit(solution)/shard_map/broadcast_in_dim | solution.py:73
  51.2 0.0 copy-done.3
  51.2 18.8 %while.13 = (s32[]{:T(128)}, bf16[12,192,128]{2,0,1:T(8,128)(2,1)}, f32[12,192,128]{2,1,0:T(8,128)}, pred[192]{0:T(512)(128)(4,1)S(1)}, bf16[12,192,4,32]{1,3,2,...) while((s32[]{:T(128)}, bf16[12,192,128]{2,0,1:T(8,128)(2,1)}, ...), condition=%wide.region_5.6_spmd, body=%wide.region_2.5_spmd.sunk | while | flops 118112448 | bytes 19440052 | solution.py:69
  51.2 0.2 constant_dynamic-slice_fusion.13
  51.4 0.2 copy.80
  51.6 4.5 %fusion.59 = (f32[4,12,96]{2,1,0:T(8,128)S(1)}, bf16[4,12,96,192]{3,2,1,0:T(8,128)(2,1)}) fusion(f32[4,96,192]{2,1,0:T(8,128)S(1)} %copy.80, pred[192]{0:T(512)(128)(4,1)S(1)} %get-tuple-element.270, bf16[12,192,4,32]{1,3,0,2:T(8,128)(2,1)S(1)} %get-tuple-element.272, bf16[12,192,4,32]{1,3,2,0:T(8,128)(2,1)} %get-tuple-element.271, s32[]{:T(128)S(6)} %select_n.31), kind=kOutput, calls=%fused_computation.43.clone.1 | convolution fusion | flops 61046976 | bytes 3066052 | tf_op jit(solution)/shard_map/while/body/eval_jaxpr/sub | solution.py:61
  56.1 0.0 copy-start.2
  56.1 2.9 %fusion.60 = f32[12,96,4,32]{1,3,2,0:T(8,128)S(1)} fusion(bf16[12,192,4,32]{1,3,2,0:T(8,128)(2,1)} %get-tuple-element.274, bf16[4,12,96,192]{3,2,1,0:T(8,128)(2,1)} %get-tuple-element.241, f32[12,96,4]{1,2,0:T(4,128)S(1)} %copy.81), kind=kOutput, calls=%fused_computation.10.clone.1 | convolution fusion | flops 56770560 | bytes 2967552 | tf_op jit(solution)/shard_map/while/body/eval_jaxpr/hijk,ikhd->ijhd/dot_general | solution.py:64
  59.0 0.0 copy-done.2
  59.0 0.1 constant_dynamic-slice_fusion.12
  59.0 0.3 copy.79
  59.3 0.1 fusion.61
  59.4 0.4 copy.82
  59.8 0.8 constant_dynamic-update-slice_fusion.2
  60.6 0.2 constant_dynamic-slice_fusion.13
  60.8 0.2 copy.80
  61.0 4.5 %fusion.59 = (f32[4,12,96]{2,1,0:T(8,128)S(1)}, bf16[4,12,96,192]{3,2,1,0:T(8,128)(2,1)}) fusion(f32[4,96,192]{2,1,0:T(8,128)S(1)} %copy.80, pred[192]{0:T(512)(128)(4,1)S(1)} %get-tuple-element.270, bf16[12,192,4,32]{1,3,0,2:T(8,128)(2,1)S(1)} %get-tuple-element.272, bf16[12,192,4,32]{1,3,2,0:T(8,128)(2,1)} %get-tuple-element.271, s32[]{:T(128)S(6)} %select_n.31), kind=kOutput, calls=%fused_computation.43.clone.1 | convolution fusion | flops 61046976 | bytes 3066052 | tf_op jit(solution)/shard_map/while/body/eval_jaxpr/sub | solution.py:61
  65.5 0.0 copy-start.2
  65.5 2.9 %fusion.60 = f32[12,96,4,32]{1,3,2,0:T(8,128)S(1)} fusion(bf16[12,192,4,32]{1,3,2,0:T(8,128)(2,1)} %get-tuple-element.274, bf16[4,12,96,192]{3,2,1,0:T(8,128)(2,1)} %get-tuple-element.241, f32[12,96,4]{1,2,0:T(4,128)S(1)} %copy.81), kind=kOutput, calls=%fused_computation.10.clone.1 | convolution fusion | flops 56770560 | bytes 2967552 | tf_op jit(solution)/shard_map/while/body/eval_jaxpr/hijk,ikhd->ijhd/dot_general | solution.py:64
  68.4 0.1 constant_dynamic-slice_fusion.12
  68.4 0.3 copy.79
  68.7 0.1 fusion.61
  68.8 0.4 copy.82
  69.2 0.8 constant_dynamic-update-slice_fusion.2
  70.0 15.2 %all_to_all.41 = bf16[12,192,128]{2,0,1:T(8,128)(2,1)S(1)} all-to-all(bf16[12,192,128]{2,0,1:T(8,128)(2,1)} %get-tuple-element.282), channel_id=1, replica_groups=mesh['groups'=2,'rows'=4,'cols'=4] {'rows'}, dimensions={1} | all-to-all | bytes 1179648 | tf_op jit(solution)/shard_map/all_to_all | solution.py:75
  85.2 0.2 copy.46
  85.4 1.3 %convolution_add_fusion = f32[48,48,128]{2,1,0:T(8,128)} fusion(bf16[48,48,128]{2,1,0:T(8,128)(2,1)S(1)} %bitcast.66, f32[128]{0:T(128)S(1)} %copy-done.10, bf16[128,128]{1,0:T(8,128)(2,1)S(1)} %copy-done.5), kind=kOutput, calls=%fused_computation.23 | convolution fusion | flops 75792384 | bytes 1802752 | tf_op jit(solution)/shard_map/dot_general | solution.py:76
  (23 shorter events, 0.1 us)
Async XLA Ops:
  0.0 38.6 %copy-start = (bf16[128,256]{1,0:T(8,128)(2,1)S(1)}, bf16[128,256]{1,0:T(8,128)(2,1)}, u32[]{:S(2)}) copy-start(bf16[128,256]{1,0:T(8,128)(2,1)} %param.18) | copy-start | bytes 196612
  0.0 1.8 %copy-start.1 = (f32[48,48,128]{2,1,0:T(8,128)S(1)}, f32[48,48,128]{2,1,0:T(8,128)}, u32[]{:S(2)}) copy-start(f32[48,48,128]{2,1,0:T(8,128)} %param.13) | copy-start | bytes 3538948
  0.0 2.5 %copy-start.9 = (f32[128]{0:T(128)S(1)}, f32[128]{0:T(128)}, u32[]{:S(2)}) copy-start(f32[128]{0:T(128)} %param.15) | copy-start | bytes 1540
  0.0 2.5 %copy-start.8 = (f32[128]{0:T(128)S(1)}, f32[128]{0:T(128)}, u32[]{:S(2)}) copy-start(f32[128]{0:T(128)} %param.16) | copy-start | bytes 1540
  2.5 5.8 %copy-start.7 = (f32[128,4]{0,1:T(4,128)S(1)}, f32[128,4]{0,1:T(4,128)}, u32[]{:S(2)}) copy-start(f32[128,4]{0,1:T(4,128)} %param.21) | copy-start | bytes 6148
  4.0 30.0 %all-to-all-start = ((bf16[48,48,128]{2,1,0:T(8,128)(2,1)}), bf16[48,48,128]{2,1,0:T(8,128)(2,1)S(1)}, u32[]{:S(2)}, u32[]{:S(2)}) async-start(bf16[48,48,128]{2,1,0:T(8,128)(2,1)} %add_convert_fusion), calls=%async_computation | async-start | bytes 1179648 | tf_op jit(solution)/shard_map/all_to_all | solution.py:30
  8.3 18.9 %copy-start.14 = (u32[32]{0:T(128)S(1)}, u32[32]{0:T(128)}, u32[]{:S(2)}) copy-start(u32[32]{0:T(128)} %constant.66) | copy-start | bytes 388
  8.3 20.0 %copy-start.12 = (s32[48]{0:T(128)S(1)}, s32[48]{0:T(128)}, u32[]{:S(2)}) copy-start(s32[48]{0:T(128)} %param.14) | copy-start | bytes 580
  35.0 15.1 %all-to-all-start.1 = ((f32[4,4,192,48]{2,3,1,0:T(8,128)}), f32[4,4,192,48]{2,3,1,0:T(8,128)S(1)}, u32[]{:S(2)}, u32[]{:S(2)}) async-start(f32[4,4,192,48]{2,3,1,0:T(8,128)} %stack.2), calls=%async_computation.1 | async-start | bytes 1572864 | tf_op jit(solution)/shard_map/all_to_all | solution.py:35
  41.5 2.1 %copy-start.6 = (bf16[128,128]{1,0:T(8,128)(2,1)S(1)}, bf16[128,128]{1,0:T(8,128)(2,1)}, u32[]{:S(2)}) copy-start(bf16[128,128]{1,0:T(8,128)(2,1)} %param.17) | copy-start | bytes 98308
  43.7 1.5 %copy-start.11 = (bf16[128,128]{1,0:T(8,128)(2,1)S(1)}, bf16[128,128]{1,0:T(8,128)(2,1)}, u32[]{:S(2)}) copy-start(bf16[128,128]{1,0:T(8,128)(2,1)} %param.19) | copy-start | bytes 98308
  43.7 1.5 %copy-start.13 = (f32[128]{0:T(128)S(1)}, f32[128]{0:T(128)}, u32[]{:S(2)}) copy-start(f32[128]{0:T(128)} %param.20) | copy-start | bytes 1540
  46.6 4.5 %copy-start.3 = (bf16[12,192,4,32]{1,3,0,2:T(8,128)(2,1)S(1)}, bf16[12,192,4,32]{1,3,0,2:T(8,128)(2,1)}, u32[]{:S(2)}) copy-start(bf16[12,192,4,32]{1,3,0,2:T(8,128)(2,1)} %copy.42) | copy-start | bytes 1769476
  56.1 2.9 %copy-start.2 = (f32[12,192,128]{2,1,0:T(8,128)S(1)}, f32[12,192,128]{2,1,0:T(8,128)}, u32[]{:S(2)}) copy-start(f32[12,192,128]{2,1,0:T(8,128)} %get-tuple-element.269) | copy-start | bytes 3538948 | tf_op jit(solution)/shard_map/while
  59.4 1.2 %copy-start.4 = (bf16[12,192,4,32]{1,3,0,2:T(8,128)(2,1)S(1)}, bf16[12,192,4,32]{1,3,0,2:T(8,128)(2,1)}, u32[]{:S(2)}) copy-start(bf16[12,192,4,32]{1,3,0,2:T(8,128)(2,1)} %get-tuple-element.293) | copy-start | bytes 1769476 | tf_op jit(solution)/shard_map/while
  65.5 2.9 %copy-start.2 = (f32[12,192,128]{2,1,0:T(8,128)S(1)}, f32[12,192,128]{2,1,0:T(8,128)}, u32[]{:S(2)}) copy-start(f32[12,192,128]{2,1,0:T(8,128)} %get-tuple-element.269) | copy-start | bytes 3538948 | tf_op jit(solution)/shard_map/while
  68.8 1.2 %copy-start.4 = (bf16[12,192,4,32]{1,3,0,2:T(8,128)(2,1)S(1)}, bf16[12,192,4,32]{1,3,0,2:T(8,128)(2,1)}, u32[]{:S(2)}) copy-start(bf16[12,192,4,32]{1,3,0,2:T(8,128)(2,1)} %get-tuple-element.293) | copy-start | bytes 1769476 | tf_op jit(solution)/shard_map/while
  70.0 15.4 %copy-start.5 = (bf16[128,128]{1,0:T(8,128)(2,1)S(1)}, bf16[128,128]{1,0:T(8,128)(2,1)}, u32[]{:S(2)}) copy-start(bf16[128,128]{1,0:T(8,128)(2,1)} %param.22) | copy-start | bytes 98308
  70.0 15.4 %copy-start.10 = (f32[128]{0:T(128)S(1)}, f32[128]{0:T(128)}, u32[]{:S(2)}) copy-start(f32[128]{0:T(128)} %param.23) | copy-start | bytes 1540
